TPU v7x, 32 devices: a whole 2x2x4 slice. The times are simulated.
32 devices in a mesh: sub: 4 (over z), row: 2 (over core), col: 4 (over y, x).
Axes of the slice: x: 2, y: 2, z: 4, core: 2. Of those that a mesh axis runs over, the one named last changes fastest.
Arguments:
- factor_cols: bfloat16 [4, 2, 2048, 4096], P('sub', None, 'col', 'row'), may hold values from -0.09375 to 0.09375
- block_pattern: int32 [4, 16, 16], P('sub'), may hold values 0 or 1
- diag_inverse: float32 [4, 4096, 2048], P('sub', ('row', 'col')), may hold values from -1 to 2
- coupling_cols: bfloat16 [4, 2, 2048, 1024], P('sub', 'row', 'col'), may hold values from -0.09375 to 0.09375
- separator_rows: int32 [4, 1024], P('sub'), may hold values from 0 to 1535, as said below
- root_inverse: float32 [1536, 1536], P('col'), may hold values from -1 to 2
- right_side: float32 [4, 4096, 128], P('sub', 'row'), may hold values from -6 to 6
- root_right: float32 [1536, 128], P('col'), may hold values from -6 to 6
Outputs:
- solution: float32 [4, 4096, 128], P('sub', ('row', 'col'))
- root_solution: float32 [1536, 128], P('col')
Inputs may be any that keep to these rules, and one draw needn't show every extreme that they name: `separator_rows`: within one section the 1024 entries are distinct.
All inputs are finite; a program needn't handle non-finite values. No bound on the sum of `block_pattern` on one device may be relied on, other than what follows from the above.
Results may differ from a plain program's by a relative error of at most 0.003.
Values may be sent and summed in bfloat16 or wider, within the bound.
A program may use at most 64 MiB of HBM per device.

v0:
```python
import jax
import jax.numpy as jnp
from jax import lax
from jax.sharding import PartitionSpec as P

BLOCK = 256
SEPARATOR = 1536


precise = lax.Precision.HIGHEST
first_axes = (((0,), (0,)), ((), ()))


def spread(block, axis, source):
    block = jnp.where(lax.axis_index(axis) == source, block, jnp.zeros_like(block))
    return lax.psum(block, axis)


def shards(
    factor_cols,
    block_pattern,
    diag_inverse,
    coupling_cols,
    separator_rows,
    root_inverse,
    right_side,
    root_right,
):
    factor = factor_cols[0]
    table = block_pattern[0]
    inverse = diag_inverse[0]
    couple_own = coupling_cols[0, 0]
    right_rows = right_side[0]
    rows_sep = separator_rows[0]
    panel_count, col_width, panel_rows = factor.shape
    sources = right_rows.shape[1]
    block_count = table.shape[1]
    row_id = lax.axis_index("row")
    col_id = lax.axis_index("col")
    sub_id = lax.axis_index("sub")
    own_blocks = lax.dynamic_slice_in_dim(
        table, row_id * (panel_rows // BLOCK), panel_rows // BLOCK, 0
    ).astype(jnp.float32)
    row_mask = jnp.repeat(own_blocks, BLOCK, axis=0)
    col_pos = (
        jnp.arange(panel_count)[:, None] * panel_rows
        + col_id * col_width
        + jnp.arange(col_width)[None, :]
    )
    selector = (jnp.arange(block_count)[:, None, None] == (col_pos // BLOCK)[None]).astype(
        jnp.float32
    )
    pattern_mask = jnp.einsum("in,nqj->qji", row_mask, selector)
    below_mask = (jnp.arange(panel_count) < row_id).astype(jnp.float32)[:, None, None]
    masked = factor * (pattern_mask * below_mask).astype(jnp.bfloat16)
    zero_panel = jnp.zeros((panel_rows, sources), jnp.float32)
    zero_share = jnp.zeros((col_width, sources), jnp.float32)

    def forward(current, carried):
        accumulated, solved = carried
        panel_total = lax.psum(accumulated, "col")
        solved = lax.cond(
            row_id == current,
            lambda values: jnp.dot(
                inverse, right_rows - values, precision=precise, preferred_element_type=jnp.float32
            ),
            lambda values: solved,
            panel_total,
        )
        received = spread(solved.astype(jnp.bfloat16), "row", current)
        factor_now = lax.dynamic_index_in_dim(masked, current, 0, keepdims=False)
        accumulated = accumulated + lax.dot_general(
            factor_now, received, first_axes, preferred_element_type=jnp.float32
        )
        return (accumulated, solved)

    accumulated, solved = lax.fori_loop(0, panel_count, forward, (zero_panel, zero_share))
    own_low = solved.astype(jnp.bfloat16)
    sep_partial = lax.dot_general(
        couple_own, own_low, first_axes, preferred_element_type=jnp.float32
    )
    onehot = (jnp.arange(SEPARATOR)[:, None] == rows_sep[None, :]).astype(jnp.float32)
    mapped = jnp.dot(onehot, sep_partial, precision=precise, preferred_element_type=jnp.float32)
    share_rows = root_inverse.shape[0]
    slice_start = col_id * share_rows
    first_device = ((sub_id == 0) & (row_id == 0)).astype(jnp.float32)
    own_rows = (
        lax.dynamic_slice_in_dim(-mapped, slice_start, share_rows, 0) + first_device * root_right
    )
    root_term = lax.dynamic_update_slice_in_dim(-mapped, own_rows, slice_start, 0)
    root_share = lax.psum_scatter(root_term, "col", scatter_dimension=0, tiled=True)
    root_share = lax.psum(root_share, ("sub", "row"))
    root_rhs = lax.all_gather(root_share, "col", axis=0, tiled=True)
    root_half = jnp.dot(
        root_inverse, root_rhs, precision=precise, preferred_element_type=jnp.float32
    )
    root_part = lax.psum_scatter(
        lax.dot_general(
            root_inverse,
            root_half,
            first_axes,
            precision=precise,
            preferred_element_type=jnp.float32,
        ),
        "col",
        scatter_dimension=0,
        tiled=True,
    )
    root_full = lax.all_gather(root_part.astype(jnp.bfloat16), "col", axis=0, tiled=True).astype(
        root_part.dtype
    )
    picked = lax.dot_general(
        onehot, root_full, first_axes, precision=precise, preferred_element_type=jnp.float32
    ).astype(jnp.bfloat16)
    couple_back = jnp.dot(couple_own, picked, preferred_element_type=jnp.float32)

    def backward(counter, carried):
        finished, panel_low = carried
        current = panel_count - 1 - counter
        factor_now = lax.dynamic_index_in_dim(masked, current, 0, keepdims=False)
        contribution = jnp.dot(factor_now, panel_low, preferred_element_type=jnp.float32)
        own_couple = couple_back * (row_id == current).astype(jnp.float32)
        summed = lax.psum(contribution + own_couple, "row")
        partial_value = lax.cond(
            row_id == current,
            lambda values: lax.dot_general(
                inverse,
                solved - values,
                first_axes,
                precision=precise,
                preferred_element_type=jnp.float32,
            ),
            lambda values: zero_panel,
            summed,
        )
        value = lax.psum_scatter(partial_value, "col", scatter_dimension=0, tiled=True)
        whole_low = lax.all_gather(value.astype(jnp.bfloat16), "col", axis=0, tiled=True)
        active = row_id == current
        finished = jnp.where(active, value, finished)
        panel_low = jnp.where(active, whole_low, panel_low)
        return (finished, panel_low)

    finished, panel_low = lax.fori_loop(
        0, panel_count, backward, (zero_share, zero_panel.astype(jnp.bfloat16))
    )
    return (finished[None], root_part)


def solution(mesh):
    return jax.shard_map(
        shards,
        mesh=mesh,
        in_specs=(
            P("sub", None, "col", "row"),
            P("sub", None, None),
            P("sub", ("row", "col"), None),
            P("sub", "row", "col", None),
            P("sub", None),
            P("col", None),
            P("sub", "row", None),
            P("col", None),
        ),
        out_specs=(P("sub", ("row", "col"), None), P("col", None)),
        check_vma=False,
    )
```

profile of v0, /device:TPU:0, one launch (start us, length us, event | category | flops | bytes accessed | tf_op | source)
XLA Modules:
  0.0 492.3 jit_solution(17336748662876805987)
XLA Ops:
  8.0 0.8 convert_bitcast_fusion
  8.9 0.1 copy.10
  9.0 0.1 broadcast_in_dim.25
  9.1 0.1 and_select_fusion
  9.2 5.5 %bitcast_multiply_fusion = bf16[2,512,2048]{2,1,0:T(8,128)(2,1)} fusion(bf16[1,2,512,2048]{3,2,1,0:T(8,128)(2,1)} %param.16, f32[2]{0:T(128)S(1)} %compare_convert_fusion, bf16[2048,16,1]{0,1,2:T(8,128)(2,1)S(1)} %reshape.56, s32[2,512]{1,0:T(2,128)S(1)} %and_select_fusion), kind=kOutput, calls=%fused_computation.24 | convolution fusion | flops 73416704 | bytes 8458248 | tf_op jit(solution)/shard_map/in,nqj->qji/dot_general | solution.py:53
  14.7 0.7 broadcast_in_dim.23
  15.4 178.1 %while.37 = (s32[]{:T(128)}, f32[2048,128]{1,0:T(8,128)}, f32[512,128]{0,1:T(8,128)}, bf16[2,512,2048]{2,1,0:T(8,128)(2,1)}, s32[]{:T(128)}, /*index=5*/f32[2048...) while((s32[]{:T(128)}, f32[2048,128]{1,0:T(8,128)}, ...), condition=%wide.region_5.6_spmd.clone, body=%wide.region_0.5_spmd.clone.sunk | while | flops 1880293376 | bytes 24641860 | solution.py:77
  15.4 1.0 broadcast_select_fusion.7
  16.5 0.0 all-reduce.9.cloned.1.call-start
  16.6 58.0 %all-reduce.7.cloned.1.call-done = f32[2048,128]{1,0:T(8,128)} async-done(((f32[2048,128]{1,0:T(8,128)}), f32[2048,128]{1,0:T(8,128)}) %all-reduce.7.cloned.1.call-update) | async-done | bytes 1048592 | tf_op jit(solution)/shard_map/while/body/eval_jaxpr/psum | solution.py:61
  74.5 8.0 %conditional.7 = (f32[512,128]{0,1:T(8,128)}) conditional(s32[]{:T(128)} %convert_element_type.111, f32[512,128]{0,1:T(8,128)} %get-tuple-element.579, (f32[2048,128]{1,0:T(8,128)}, f32[2048,128]{1,0:T(8,128)}, f32[512,2048]{1,0:T(8,128)}) %tuple.109), branch_computations={%region_2.2_spmd.clone, %region_3.3_spmd.clone} | conditional | flops 1610874880 | bytes 6553608
  74.5 8.0 %convolution_bitcast_fusion.1 = f32[512,128]{0,1:T(8,128)} fusion(f32[512,2048]{1,0:T(8,128)} %get-tuple-element.370, f32[2048,128]{1,0:T(8,128)} %get-tuple-element.368, f32[2048,128]{1,0:T(8,128)} %get-tuple-element.369), kind=kOutput, calls=%fused_computation.2 | convolution fusion | flops 1610874880 | bytes 6553600 | tf_op jit(solution)/shard_map/while/body/eval_jaxpr/cond/branch_1_fun/dot_general | solution.py:64
  82.6 1.6 convert_select_fusion.2
  84.2 18.1 %all-reduce.9.cloned.1.call-done = bf16[512,128]{0,1:T(8,128)(2,1)} async-done(((bf16[512,128]{0,1:T(8,128)(2,1)}), bf16[512,128]{0,1:T(8,128)(2,1)}) %all-reduce.9.cloned.1.call-update) | async-done | bytes 131088 | tf_op jit(solution)/shard_map/while/body/eval_jaxpr/psum | solution.py:16
  102.3 3.3 convolution_add_fusion.2
  105.6 2.3 broadcast_select_fusion.7
  107.9 0.0 all-reduce.9.cloned.1.call-start
  108.0 55.2 %all-reduce.7.cloned.1.call-done = f32[2048,128]{1,0:T(8,128)} async-done(((f32[2048,128]{1,0:T(8,128)}), f32[2048,128]{1,0:T(8,128)}) %all-reduce.7.cloned.1.call-update) | async-done | bytes 1048592 | tf_op jit(solution)/shard_map/while/body/eval_jaxpr/psum | solution.py:61
  163.2 1.6 convert_select_fusion.2
  164.8 25.4 %all-reduce.9.cloned.1.call-done = bf16[512,128]{0,1:T(8,128)(2,1)} async-done(((bf16[512,128]{0,1:T(8,128)(2,1)}), bf16[512,128]{0,1:T(8,128)(2,1)}) %all-reduce.9.cloned.1.call-update) | async-done | bytes 131088 | tf_op jit(solution)/shard_map/while/body/eval_jaxpr/psum | solution.py:16
  190.2 3.3 convolution_add_fusion.2
  193.6 1.6 fusion.25
  195.2 2.9 fusion.20
  198.2 0.9 copy-done.5
  199.1 0.0 reduce-scatter.4.cloned.1.call-update
  199.2 0.0 all-reduce.5.cloned.1.call-start
  199.2 27.3 %reduce-scatter.4.cloned.1.call-done = f32[384,128]{1,0:T(8,128)} async-done(((f32[1536,128]{1,0:T(8,128)}), f32[384,128]{1,0:T(8,128)}) %reduce-scatter.4.cloned.1.call-update) | async-done | bytes 196624 | tf_op jit(solution)/shard_map/reduce_scatter | solution.py:91
  226.5 0.0 all-reduce.5.cloned.1.call-update
  226.5 0.0 reduce-scatter.6.cloned.1.call-start
  226.6 57.1 %all-reduce.5.cloned.1.call-done = f32[384,128]{1,0:T(8,128)} async-done(((f32[384,128]{1,0:T(8,128)}), f32[384,128]{1,0:T(8,128)}) %all-reduce.5.cloned.1.call-update) | async-done | bytes 196624 | tf_op jit(solution)/shard_map/psum | solution.py:92
  283.7 12.6 %all_gather.16 = f32[1536,128]{1,0:T(8,128)S(1)} all-gather(f32[384,128]{1,0:T(8,128)} %all-reduce.5.cloned.1.call-done), channel_id=1, replica_groups=mesh['sub'=4,'row'=2,'col'=4] {'col'}, dimensions={0}, use_global_device_ids=true | all-gather | bytes 983040 | tf_op jit(solution)/shard_map/all_gather | solution.py:93
  296.3 2.9 fusion.30
  299.2 2.5 convolution_bitcast_fusion.2
  301.7 0.0 reduce-scatter.6.cloned.1.call-update
  301.7 0.8 copy.12
  302.5 23.4 %reduce-scatter.6.cloned.1.call-done = f32[384,128]{0,1:T(8,128)} async-done(((f32[1536,128]{0,1:T(8,128)}), f32[384,128]{0,1:T(8,128)}) %reduce-scatter.6.cloned.1.call-update) | async-done | bytes 196624 | tf_op jit(solution)/shard_map/reduce_scatter | solution.py:97
  326.0 0.9 convert_element_type.87
  326.9 10.2 %all_gather.17 = bf16[1536,128]{0,1:T(8,128)(2,1)S(1)} all-gather(bf16[384,128]{0,1:T(8,128)(2,1)S(1)} %convert_element_type.87), channel_id=1, replica_groups=mesh['sub'=4,'row'=2,'col'=4] {'col'}, dimensions={0}, use_global_device_ids=true | all-gather | bytes 491520 | tf_op jit(solution)/shard_map/all_gather | solution.py:109
  337.1 1.0 fusion.21
  338.1 1.2 convolution_bitcast_fusion.3
  339.3 1.8 copy.11
  341.1 140.1 %while.38 = (s32[]{:T(128)}, f32[512,128]{0,1:T(8,128)}, bf16[2048,128]{0,1:T(8,128)(2,1)}, s32[]{:T(128)}, bf16[2,512,2048]{2,1,0:T(8,128)(2,1)}, /*index=5*/f3...) while((s32[]{:T(128)}, f32[512,128]{0,1:T(8,128)}, ...), condition=%wide.region_14.15_spmd.clone, body=%wide.region_9.14_spmd.clone.sunk | while | flops 1880293376 | bytes 21758288 | solution.py:143
  341.1 3.0 fusion.50
  344.1 0.0 reduce-scatter.8.cloned.1.call-start
  344.2 18.6 %all-reduce.11.cloned.1.call-done = f32[512,128]{1,0:T(8,128)} async-done(((f32[512,128]{1,0:T(8,128)}), f32[512,128]{1,0:T(8,128)}) %all-reduce.11.cloned.1.call-update) | async-done | bytes 262160 | tf_op jit(solution)/shard_map/while/body/eval_jaxpr/psum | solution.py:123
  362.8 0.1 conditional.8
  362.8 0.1 broadcast_in_dim.1
  362.9 1.0 copy-done.2
  363.9 33.8 %reduce-scatter.8.cloned.1.call-done = f32[512,128]{0,1:T(8,128)} async-done(((f32[2048,128]{0,1:T(8,128)}), f32[512,128]{0,1:T(8,128)}) %reduce-scatter.8.cloned.1.call-update) | async-done | bytes 262160 | tf_op jit(solution)/shard_map/while/body/eval_jaxpr/reduce_scatter | solution.py:136
  397.7 1.8 fusion.51
  399.4 10.1 %all_gather.20 = bf16[2048,128]{0,1:T(8,128)(2,1)S(1)} all-gather(bf16[512,128]{0,1:T(8,128)(2,1)S(1)} %get-tuple-element.563), channel_id=1, replica_groups=mesh['sub'=4,'row'=2,'col'=4] {'col'}, dimensions={0}, use_global_device_ids=true | all-gather | bytes 655360 | tf_op jit(solution)/shard_map/while/body/eval_jaxpr/all_gather | solution.py:137
  409.5 0.9 broadcast_select_fusion.9
  410.4 3.2 fusion.50
  413.6 0.0 reduce-scatter.8.cloned.1.call-start
  413.6 18.7 %all-reduce.11.cloned.1.call-done = f32[512,128]{1,0:T(8,128)} async-done(((f32[512,128]{1,0:T(8,128)}), f32[512,128]{1,0:T(8,128)}) %all-reduce.11.cloned.1.call-update) | async-done | bytes 262160 | tf_op jit(solution)/shard_map/while/body/eval_jaxpr/psum | solution.py:123
  432.3 4.7 conditional.8
  432.3 4.7 convolution_bitcast_fusion
  437.0 1.0 copy-done.2
  438.0 29.3 %reduce-scatter.8.cloned.1.call-done = f32[512,128]{0,1:T(8,128)} async-done(((f32[2048,128]{0,1:T(8,128)}), f32[512,128]{0,1:T(8,128)}) %reduce-scatter.8.cloned.1.call-update) | async-done | bytes 262160 | tf_op jit(solution)/shard_map/while/body/eval_jaxpr/reduce_scatter | solution.py:136
  467.3 1.9 fusion.51
  469.2 10.0 %all_gather.20 = bf16[2048,128]{0,1:T(8,128)(2,1)S(1)} all-gather(bf16[512,128]{0,1:T(8,128)(2,1)S(1)} %get-tuple-element.563), channel_id=1, replica_groups=mesh['sub'=4,'row'=2,'col'=4] {'col'}, dimensions={0}, use_global_device_ids=true | all-gather | bytes 655360 | tf_op jit(solution)/shard_map/while/body/eval_jaxpr/all_gather | solution.py:137
  479.3 1.9 broadcast_select_fusion.9
  481.2 1.8 copy.13
  483.0 1.7 copy.14
  (38 shorter events, 0.3 us)
Async XLA Ops:
  8.0 288.3 %copy-start = (f32[384,1536]{1,0:T(8,128)S(1)}, f32[384,1536]{1,0:T(8,128)}, u32[]{:S(2)}) copy-start(f32[384,1536]{1,0:T(8,128)} %param.21) | copy-start | bytes 7077892
  15.4 179.8 %copy-start.7 = (s32[1,1024]{1,0:T(1,128)S(1)}, s32[1,1024]{1,0:T(1,128)}, u32[]{:S(2)}) copy-start(s32[1,1024]{1,0:T(1,128)} %param.20) | copy-start | bytes 12292
  15.4 59.1 %all-reduce.7.cloned.1.call-start = ((), (), s32[]{:S(2)}) async-start(), calls=%async_computation.6 | async-start | bytes 2097152 | tf_op jit(solution)/shard_map/while/body/eval_jaxpr/psum | solution.py:61
  16.5 85.8 %copy-start.1 = (f32[2048,128]{1,0:T(8,128)S(1)}, f32[2048,128]{1,0:T(8,128)}, u32[]{:S(2)}) copy-start(f32[2048,128]{1,0:T(8,128)} %broadcast_select_fusion.7) | copy-start | bytes 3145732 | tf_op jit(solution)/shard_map/while
  16.5 85.8 %all-reduce.9.cloned.1.call-start = ((), (), s32[]{:S(2)}) async-start(), calls=%async_computation.7 | async-start | bytes 262144 | tf_op jit(solution)/shard_map/while/body/eval_jaxpr/psum | solution.py:16
  105.6 57.6 %all-reduce.7.cloned.1.call-start = ((), (), s32[]{:S(2)}) async-start(), calls=%async_computation.6 | async-start | bytes 2097152 | tf_op jit(solution)/shard_map/while/body/eval_jaxpr/psum | solution.py:61
  107.9 82.4 %copy-start.1 = (f32[2048,128]{1,0:T(8,128)S(1)}, f32[2048,128]{1,0:T(8,128)}, u32[]{:S(2)}) copy-start(f32[2048,128]{1,0:T(8,128)} %broadcast_select_fusion.7) | copy-start | bytes 3145732 | tf_op jit(solution)/shard_map/while
  107.9 82.3 %all-reduce.9.cloned.1.call-start = ((), (), s32[]{:S(2)}) async-start(), calls=%async_computation.7 | async-start | bytes 262144 | tf_op jit(solution)/shard_map/while/body/eval_jaxpr/psum | solution.py:16
  193.6 4.6 copy-start.6
  193.6 32.9 %reduce-scatter.4.cloned.1.call-start = ((), (), s32[]{:S(2)}) async-start(), calls=%async_computation.3 | async-start | bytes 983040 | tf_op jit(solution)/shard_map/reduce_scatter | solution.py:91
  198.2 0.9 copy-start.5
  199.2 84.6 %all-reduce.5.cloned.1.call-start = ((), (), s32[]{:S(2)}) async-start(), calls=%async_computation.4 | async-start | bytes 393216 | tf_op jit(solution)/shard_map/psum | solution.py:92
  226.5 75.2 %copy-start.3 = (f32[512,128]{0,1:T(8,128)S(1)}, f32[512,128]{0,1:T(8,128)}, u32[]{:S(2)}) copy-start(f32[512,128]{0,1:T(8,128)} %get-tuple-element.430) | copy-start | bytes 786436
  226.5 99.4 %reduce-scatter.6.cloned.1.call-start = ((), (), s32[]{:S(2)}) async-start(), calls=%async_computation.5 | async-start | bytes 983040 | tf_op jit(solution)/shard_map/reduce_scatter | solution.py:97
  302.5 35.6 %copy-start.4 = (bf16[1,1,512,1024]{3,2,1,0:T(8,128)(2,1)S(1)}, bf16[1,1,512,1024]{3,2,1,0:T(8,128)(2,1)}, u32[]{:S(2)}) copy-start(bf16[1,1,512,1024]{3,2,1,0:T(8,128)(2,1)} %param.19) | copy-start | bytes 3145732
  341.1 21.6 %all-reduce.11.cloned.1.call-start = ((), (), s32[]{:S(2)}) async-start(), calls=%async_computation.8 | async-start | bytes 524288 | tf_op jit(solution)/shard_map/while/body/eval_jaxpr/psum | solution.py:123
  344.1 53.5 %reduce-scatter.8.cloned.1.call-start = ((), (), s32[]{:S(2)}) async-start(), calls=%async_computation.9 | async-start | bytes 1310720 | tf_op jit(solution)/shard_map/while/body/eval_jaxpr/reduce_scatter | solution.py:136
  362.9 1.0 copy-start.2
  410.4 21.9 %all-reduce.11.cloned.1.call-start = ((), (), s32[]{:S(2)}) async-start(), calls=%async_computation.8 | async-start | bytes 524288 | tf_op jit(solution)/shard_map/while/body/eval_jaxpr/psum | solution.py:123
  413.6 53.8 %reduce-scatter.8.cloned.1.call-start = ((), (), s32[]{:S(2)}) async-start(), calls=%async_computation.9 | async-start | bytes 1310720 | tf_op jit(solution)/shard_map/while/body/eval_jaxpr/reduce_scatter | solution.py:136
  437.0 1.0 copy-start.2
Sparse Core Ops, SparseCore 0:
  19.3 55.1 all-reduce.6
  84.3 17.9 all-reduce.8
  109.5 53.6 all-reduce.6
  165.9 24.2 all-reduce.8
  344.5 18.2 all-reduce.10
  365.5 32.1 reduce-scatter.7
  414.1 18.1 all-reduce.10
  438.1 29.1 reduce-scatter.7
Sparse Core Ops, SparseCore 1:
  199.2 27.2 reduce-scatter.3
  228.7 55.0 all-reduce.4
  301.8 24.2 reduce-scatter.5
where the time goes:
time: 493 us; the launch traced here: 492 us
  waiting for transfers between devices  365 us (74%)
  matrix products  43.2 us (9%)
  blocking collectives  42.9 us (9%)
  between operations  15.8 us (3%)
  other arithmetic  14.9 us (3%)
  local copies, waits for them, and re-layouts  10 us (2%)
    psum x2, waiting for transfers between devices, forward(): panel_total = lax.psum(accumulated, 'col')  113 us
    reduce_scatter x2, waiting for transfers between devices, backward(): lax.psum_scatter(partial_value, 'col', scatter_dimension=0, tiled=True)  63.1 us
    psum x1, waiting for transfers between devices, shards(): root_share = lax.psum(root_share, ('sub', 'row'))  57.1 us
    psum x2, waiting for transfers between devices, spread(): return lax.psum(block, axis)  43.5 us
    psum x2, waiting for transfers between devices, backward(): summed = lax.psum(contribution + own_couple, 'row')  37.3 us
    reduce_scatter x1, waiting for transfers between devices, shards(): lax.psum_scatter(root_term, 'col', scatter_dimension=0, tiled=True)  27.3 us
    reduce_scatter x1, waiting for transfers between devices, shards(): lax.psum_scatter(lax.dot_general(root_inverse, root_half, first_axes, pre...  23.4 us
    all_gather x2, blocking collectives, backward(): lax.all_gather(value.astype(jnp.bfloat16), 'col', axis=0, tiled=True)  20.1 us
  transfers between devices with their start and end apart: 11, of which 11 were waited for; matrix products, arithmetic and copies ran while one was open for 0% of the time, Pallas kernels for 0%

commit v1 on v0

v1 whole, which is shorter than its diff:
```python
import functools

import jax
import jax.numpy as jnp
from jax import lax
from jax.experimental import pallas as pl
from jax.experimental.pallas import tpu as pltpu
from jax.sharding import PartitionSpec as P

BLOCK = 256
F32 = jnp.float32
BF16 = jnp.bfloat16
ROOT_TYPE = BF16


def mm(a, b):
    return lax.dot_general(a, b, (((1,), (0,)), ((), ())), preferred_element_type=F32)


def mm_nt(a, b):
    return lax.dot_general(a, b, (((1,), (1,)), ((), ())), preferred_element_type=F32)


def halves(x):
    high = x.astype(BF16)
    low = (x - high.astype(F32)).astype(BF16)
    return high, low


def paired(x):
    return jnp.concatenate(halves(x), axis=1)


def mm_paired(high, low, pair):
    both = mm(high, pair) + mm(low, pair)
    sources = pair.shape[1] // 2
    return both[:, :sources] + both[:, sources:]


def kernel(
    sizes,
    factor_hbm,
    pattern,
    inverse_hbm,
    couple_hbm,
    rows_ref,
    root_hbm,
    right_hbm,
    root_right,
    x_out,
    root_out,
    e_raw,
    m_raw,
    c_raw,
    r_raw,
    b_raw,
    e_hi,
    e_lo,
    et_hi,
    et_lo,
    m_mask,
    m_turn,
    spread,
    spread_turn,
    r_hi,
    r_lo,
    rt_hi,
    rt_lo,
    y_keep,
    y_low,
    y_first,
    mapped_snd,
    mapped_rcv,
    a_snd,
    a_rcv,
    a_all,
    s_snd,
    s_rcv,
    z_snd,
    z_rcv,
    rhs_all,
    t_snd,
    t_rcv,
    sep_low,
    root_keep,
    back_snd,
    back_rcv,
    x_all,
    give,
    take,
    load_sem,
    pair_snd,
    pair_rcv,
    col_snd,
    col_rcv,
    z_ssem,
    z_rsem,
):
    subs, cols = sizes
    sub = lax.axis_index("sub")
    row = lax.axis_index("row")
    col = lax.axis_index("col")
    width = e_raw.shape[0]
    panel = e_raw.shape[1]
    share = r_raw.shape[0]
    separator = r_raw.shape[1]

    def load(source, target, index):
        copy = pltpu.make_async_copy(source, target, load_sem.at[index])
        copy.start()
        return copy

    get_e = load(inverse_hbm.at[0], e_raw, 0)
    get_b = load(right_hbm.at[0], b_raw, 1)
    get_m = load(factor_hbm.at[0, 0], m_raw, 2)
    get_c = load(couple_hbm.at[0, 0], c_raw, 3)
    get_r = load(root_hbm, r_raw, 4)

    barrier = pltpu.get_barrier_semaphore()
    pl.semaphore_signal(barrier, inc=1, device_id={"row": 1 - row})
    for d in range(1, cols):
        pl.semaphore_signal(barrier, inc=1, device_id={"col": lax.rem(col + d, cols)})
    for d in range(1, subs):
        pl.semaphore_signal(barrier, inc=1, device_id={"sub": lax.rem(sub + d, subs)})
    pl.semaphore_wait(barrier, 1 + (cols - 1) + (subs - 1))

    def ahead(d):
        return lax.rem(col + d, cols)

    def behind(d):
        return lax.rem(col + cols - d, cols)

    def part(k, size):
        return pl.ds(pl.multiple_of(k * size, size), size)

    def to_pair(source, target, index):
        return pltpu.make_async_remote_copy(
            source, target, pair_snd.at[index], pair_rcv.at[index], device_id={"row": 1 - row}
        )

    def to_col(source, target, stage, d):
        return pltpu.make_async_remote_copy(
            source, target, col_snd.at[stage, d], col_rcv.at[stage, d], device_id={"col": ahead(d)}
        )

    def scatter(make, send, receive, stage):
        copies = []
        for d in range(1, cols):
            send[d] = make(ahead(d)).astype(send.dtype)
            copy = to_col(send.at[d], receive.at[d], stage, d)
            copy.start()
            copies.append(copy)
        return make(col), copies

    def gathered(own, receive, copies):
        for d, copy in zip(range(1, cols), copies):
            copy.wait_recv()
            own = own + receive[d].astype(F32)
        return own

    def share_out(buffer, place, stage):
        copies = []
        for d in range(1, cols):
            copy = to_col(buffer.at[place], buffer.at[place], stage, d)
            copy.start()
            copies.append(copy)
        return copies

    def finish(copies):
        for copy in copies:
            copy.wait_send()

    def split_inverse():
        for k in range(cols):
            e_hi[k], e_lo[k] = halves(e_raw[:, k * width : (k + 1) * width])

    def turn_inverse():
        for k in range(cols):
            et_hi[k], et_lo[k] = halves(e_raw[:, k * width : (k + 1) * width].T)

    def apply_inverse():
        total = jnp.zeros((width, b_raw.shape[1]), F32)
        for k in range(cols):
            pair = paired(b_raw[k * width : (k + 1) * width, :])
            total = total + mm_paired(e_hi[k], e_lo[k], pair)
        return total

    step = min(BLOCK, separator)

    def hits(first):
        at = lax.broadcasted_iota(jnp.int32, (step, rows_ref.shape[1]), 0) + first
        return jnp.where(at == rows_ref[...], 1.0, 0.0).astype(BF16)

    def make_spread():
        for first in range(0, separator, step):
            spread[first : first + step, :] = mm_nt(hits(first), c_raw[...]).astype(BF16)

    def make_spread_turn():
        for first in range(0, separator, step):
            spread_turn[:, first : first + step] = mm_nt(c_raw[...], hits(first)).astype(BF16)

    @pl.when(row == 0)
    def _():
        get_e.wait()
        get_b.wait()
        split_inverse()
        value = apply_inverse()
        y_keep[...] = value
        y_low[...] = value.astype(BF16)
        first = to_pair(y_low, y_first, 0)
        first.start()
        get_c.wait()
        make_spread()
        mapped_snd[...] = mm(spread[...], y_low[...])
        second = to_pair(mapped_snd, mapped_rcv, 1)
        second.start()
        make_spread_turn()
        turn_inverse()
        get_m.wait()
        get_r.wait()
        to_pair(sep_low, sep_low, 2).wait_recv()
        y_keep[...] = y_keep[...] - mm(spread_turn[...], sep_low[...])
        to_pair(root_keep, root_keep, 3).wait_recv()
        root_out[...] = root_keep[...]
        to_pair(give, take, 4).wait_recv()
        pair = paired(y_keep[...] - take[...])
        own, copies = scatter(
            lambda k: mm_paired(et_hi[k], et_lo[k], pair), back_snd, back_rcv, 4
        )
        x_out[0] = gathered(own, back_rcv, copies)
        finish(copies + [first, second])

    @pl.when(row != 0)
    def _():
        tall = min(width, BLOCK)
        get_m.wait()
        for at in range(0, width, tall):
            column = (col * width + at) // BLOCK
            for block in range(panel // BLOCK):
                present = pattern[0, panel // BLOCK + block, column].astype(F32)
                ends = slice(block * BLOCK, (block + 1) * BLOCK)
                kept = m_raw[at : at + tall, ends].astype(F32) * present
                m_raw[at : at + tall, ends] = kept.astype(BF16)
        for k in range(cols):
            piece = m_raw[:, k * width : (k + 1) * width]
            m_mask[k] = piece
            m_turn[k] = piece.astype(F32).T.astype(BF16)
        to_pair(y_low, y_first, 0).wait_recv()
        low = y_first[...]
        own, sends_a = scatter(lambda k: mm(m_turn[k], low), a_snd, a_rcv, 0)
        get_e.wait()
        get_b.wait()
        split_inverse()
        started = apply_inverse()
        own = gathered(own, a_rcv, sends_a)
        a_all[col] = own.astype(BF16)
        sends_b = share_out(a_all, col, 1)
        get_c.wait()
        make_spread()
        value = started
        for d in range(cols):
            k = behind(d)
            if d > 0:
                sends_b[d - 1].wait_recv()
            value = value - (mm(e_hi[k], a_all[k]) + mm(e_lo[k], a_all[k]))
        y_keep[...] = value
        y_low[...] = value.astype(BF16)
        to_pair(mapped_snd, mapped_rcv, 1).wait_recv()
        own_low = y_low[...]
        own, sends_c = scatter(
            lambda k: mm(spread[part(k, share), :], own_low) + mapped_rcv[part(k, share), :],
            s_snd,
            s_rcv,
            2,
        )
        get_r.wait()
        r_hi[...], r_lo[...] = halves(r_raw[...])
        for first in range(0, separator, step):
            ends = slice(first, first + step)
            rt_hi[ends, :], rt_lo[ends, :] = halves(r_raw[:, ends].T)
        own = gathered(own, s_rcv, sends_c)
        z_snd[...] = own.astype(z_snd.dtype)
        sends_z = []
        for d in range(1, subs):
            copy = pltpu.make_async_remote_copy(
                z_snd,
                z_rcv.at[d],
                z_ssem.at[d],
                z_rsem.at[d],
                device_id={"sub": lax.rem(sub + d, subs)},
            )
            copy.start()
            sends_z.append(copy)
        make_spread_turn()
        turn_inverse()
        for d, copy in zip(range(1, subs), sends_z):
            copy.wait_recv()
            own = own + z_rcv[d].astype(F32)
        rhs_all[part(col, share), :] = (root_right[...] - own).astype(rhs_all.dtype)
        sends_d = share_out(rhs_all, part(col, share), 3)
        for copy in sends_d:
            copy.wait_recv()
        if rhs_all.dtype == BF16:
            half = mm(r_hi[...], rhs_all[...]) + mm(r_lo[...], rhs_all[...])
        else:
            half = mm_paired(r_hi[...], r_lo[...], paired(rhs_all[...]))
        pair_r = paired(half)
        own, sends_e = scatter(
            lambda k: mm_paired(rt_hi[part(k, share), :], rt_lo[part(k, share), :], pair_r),
            t_snd,
            t_rcv,
            5,
        )
        own = gathered(own, t_rcv, sends_e)
        sep_low[part(col, share), :] = own.astype(BF16)
        sends_f = share_out(sep_low, part(col, share), 6)
        root_out[...] = own
        root_keep[...] = own
        third = to_pair(root_keep, root_keep, 3)
        third.start()
        for copy in sends_f:
            copy.wait_recv()
        fourth = to_pair(sep_low, sep_low, 2)
        fourth.start()
        pair = paired(y_keep[...] - mm(spread_turn[...], sep_low[...]))
        own, sends_g = scatter(
            lambda k: mm_paired(et_hi[k], et_lo[k], pair), back_snd, back_rcv, 4
        )
        own = gathered(own, back_rcv, sends_g)
        x_all[col] = own.astype(BF16)
        sends_h = share_out(x_all, col, 7)
        x_out[0] = own
        total = jnp.zeros((width, own.shape[1]), F32)
        for d in range(cols):
            k = behind(d)
            if d > 0:
                sends_h[d - 1].wait_recv()
            total = total + mm(m_mask[k], x_all[k])
        give[...] = total
        fifth = to_pair(give, take, 4)
        fifth.start()
        finish(sends_a + sends_b + sends_c + sends_z + sends_d + sends_e + sends_f + sends_g)
        finish(sends_h + [third, fourth, fifth])


def shards(
    sizes,
    factor_cols,
    block_pattern,
    diag_inverse,
    coupling_cols,
    separator_rows,
    root_inverse,
    right_side,
    root_right,
):
    subs, cols = sizes
    width, panel = diag_inverse.shape[1:]
    share, separator = root_inverse.shape
    sources = right_side.shape[2]
    coupled = coupling_cols.shape[3]
    hbm = pl.BlockSpec(memory_space=pl.ANY)
    vmem = pl.BlockSpec(memory_space=pltpu.VMEM)
    smem = pl.BlockSpec(memory_space=pltpu.SMEM)
    V = pltpu.VMEM
    tile = (cols, width, width)
    scratch = [
        V((width, panel), F32),
        V((width, panel), BF16),
        V((width, coupled), BF16),
        V((share, separator), F32),
        V((panel, sources), F32),
        V(tile, BF16),
        V(tile, BF16),
        V(tile, BF16),
        V(tile, BF16),
        V(tile, BF16),
        V(tile, BF16),
        V((separator, width), BF16),
        V((width, separator), BF16),
        V((share, separator), BF16),
        V((share, separator), BF16),
        V((separator, share), BF16),
        V((separator, share), BF16),
        V((width, sources), F32),
        V((width, sources), BF16),
        V((width, sources), BF16),
        V((separator, sources), F32),
        V((separator, sources), F32),
        V((cols, width, sources), BF16),
        V((cols, width, sources), BF16),
        V((cols, width, sources), BF16),
        V((cols, share, sources), BF16),
        V((cols, share, sources), BF16),
        V((share, sources), BF16),
        V((subs, share, sources), BF16),
        V((separator, sources), ROOT_TYPE),
        V((cols, share, sources), BF16),
        V((cols, share, sources), BF16),
        V((separator, sources), BF16),
        V((share, sources), F32),
        V((cols, width, sources), BF16),
        V((cols, width, sources), BF16),
        V((cols, width, sources), BF16),
        V((width, sources), F32),
        V((width, sources), F32),
        pltpu.SemaphoreType.DMA((5,)),
        pltpu.SemaphoreType.DMA((5,)),
        pltpu.SemaphoreType.DMA((5,)),
        pltpu.SemaphoreType.DMA((8, cols)),
        pltpu.SemaphoreType.DMA((8, cols)),
        pltpu.SemaphoreType.DMA((subs,)),
        pltpu.SemaphoreType.DMA((subs,)),
    ]
    return pl.pallas_call(
        functools.partial(kernel, sizes),
        out_shape=(
            jax.ShapeDtypeStruct((1, width, sources), F32),
            jax.ShapeDtypeStruct((share, sources), F32),
        ),
        in_specs=[hbm, smem, hbm, hbm, vmem, hbm, hbm, vmem],
        out_specs=(vmem, vmem),
        scratch_shapes=scratch,
        compiler_params=pltpu.CompilerParams(
            collective_id=0, has_side_effects=True, vmem_limit_bytes=60 * 1024 * 1024
        ),
        name="tree_solve",
    )(
        factor_cols,
        block_pattern,
        diag_inverse,
        coupling_cols,
        separator_rows,
        root_inverse,
        right_side,
        root_right,
    )


def solution(mesh):
    sizes = (mesh.shape["sub"], mesh.shape["col"])
    return jax.shard_map(
        functools.partial(shards, sizes),
        mesh=mesh,
        in_specs=(
            P("sub", None, "col", "row"),
            P("sub", None, None),
            P("sub", ("row", "col"), None),
            P("sub", "row", "col", None),
            P("sub", None),
            P("col", None),
            P("sub", "row", None),
            P("col", None),
        ),
        out_specs=(P("sub", ("row", "col"), None), P("col", None)),
        check_vma=False,
    )
```

time: 493 us -> 69.3 us (0.14)
  waiting for transfers between devices: 365 us -> 0 us
  Pallas kernels: 0 us -> 65.2 us
  matrix products: 43.2 us -> 0 us
  blocking collectives: 42.9 us -> 0 us
  between operations: 15.8 us -> 0.64 us
  other arithmetic: 14.9 us -> 0 us
  local copies, waits for them, and re-layouts: 10 us -> 3.29 us
    psum x7 -> x0, waiting for transfers between devices: 251 us -> none  [the longest x2 113 us: forward(): panel_total = lax.psum(accumulated, 'col')]
    reduce_scatter x4 -> x0, waiting for transfers between devices: 114 us -> none  [the longest x2 63.1 us: backward(): lax.psum_scatter(partial_value, 'col', scatter_dimension=0, tiled=True)]
    pallas_call x0 -> x1, Pallas kernels: none -> 65.2 us  [shards(): pl.pallas_call(functools.partial(kernel, sizes), out_shape=(jax.ShapeDtyp...]
    dot_general x13 -> x0, matrix products: 43.2 us -> none  [the longest x1 8.03 us: forward(): jnp.dot(inverse, right_rows - values, precision=precise, preferred_elemen...]
    all_gather x4 -> x0, blocking collectives: 42.9 us -> none  [the longest x2 20.1 us: backward(): lax.all_gather(value.astype(jnp.bfloat16), 'col', axis=0, tiled=True)]
    select_n x5 -> x0, other arithmetic: 6.14 us -> none  [the longest x2 3.24 us: spread(): jnp.where(lax.axis_index(axis) == source, block, jnp.zeros_like(block))]
    convert_element_type x5 -> x0, other arithmetic: 5.44 us -> none  [the longest x2 3.65 us: backward(): value.astype(jnp.bfloat16)]
  transfers between devices with their start and end apart: 11 -> 0, of which waited for: 11 -> 0; matrix products, arithmetic and copies ran while one was open for 0% -> 0% of each run, Pallas kernels for 0% -> 0%
where the time goes in v1:
time: 69.3 us; the launch traced here: 69.1 us
  Pallas kernels  65.2 us (94%)
  local copies, waits for them, and re-layouts  3.29 us (5%)
    pallas_call x1, Pallas kernels, shards(): pl.pallas_call(functools.partial(kernel, sizes), out_shape=(jax.ShapeDtyp...  65.2 us
    unnamed x2, local copies, waits for them, and re-layouts  3.29 us

profile of v1, /device:TPU:0, one launch (start us, length us, event | category | flops | bytes accessed | tf_op | source)
XLA Modules:
  0.0 69.1 jit_solution(4894325561044320465)
XLA Ops:
  0.6 65.2 %tree_solve.1 = (f32[1,512,128]{2,1,0:T(8,128)}, f32[384,128]{1,0:T(8,128)}) custom-call(bf16[1,2,512,2048]{3,2,1,0:T(8,128)(2,1)} %factor_hbm.1, s32[1,16,16]{2,1,0:T(8,128)} %pattern.1, f32[1,512,2048]{2,1,0:T(8,128)} %inverse_hbm.1, bf16[1,1,512,1024]{3,2,1,0:T(8,128)(2,1)} %couple_hbm.1, s32[1,1024]{1,0:T(1,128)} %rows_ref.1, f32[384,1536]{1,0:T(8,128)} %root_hbm.1, ...), custom_call_target="tpu_custom_call" | custom-call | tf_op jit(solution)/shard_map/tree_solve/pallas_call | solution.py:415
  65.8 1.7 %copy.12 = f32[1,512,128]{2,1,0:T(8,128)} copy(f32[1,512,128]{2,1,0:T(8,128)} %get-tuple-element.4) | data formatting | bytes 524288
  67.5 1.6 %copy.13 = f32[384,128]{1,0:T(8,128)} copy(f32[384,128]{1,0:T(8,128)} %get-tuple-element.5) | data formatting | bytes 393216

commit v2 on v1

--- a/solution.py
+++ b/solution.py
@@ -10,7 +10,7 @@
 BLOCK = 256
 F32 = jnp.float32
 BF16 = jnp.bfloat16
-ROOT_TYPE = BF16
+PIECES = 2
 
 
 def mm(a, b):
@@ -78,7 +78,8 @@
     s_rcv,
     z_snd,
     z_rcv,
-    rhs_all,
+    rhs_hi,
+    rhs_lo,
     t_snd,
     t_rcv,
     sep_low,
@@ -106,15 +107,26 @@
     separator = r_raw.shape[1]
 
     def load(source, target, index):
-        copy = pltpu.make_async_copy(source, target, load_sem.at[index])
-        copy.start()
-        return copy
-
-    get_e = load(inverse_hbm.at[0], e_raw, 0)
-    get_b = load(right_hbm.at[0], b_raw, 1)
-    get_m = load(factor_hbm.at[0, 0], m_raw, 2)
-    get_c = load(couple_hbm.at[0, 0], c_raw, 3)
-    get_r = load(root_hbm, r_raw, 4)
+        return pltpu.make_async_copy(source, target, load_sem.at[index])
+
+    get_b = load(right_hbm.at[0], b_raw, 0)
+    get_m = load(factor_hbm.at[0, 0], m_raw, 1)
+    get_c = load(couple_hbm.at[0, 0], c_raw, 2)
+    get_r = load(root_hbm, r_raw, 3)
+    get_e = []
+    for k in range(cols):
+        ends = pl.ds(k * width, width)
+        get_e.append(load(inverse_hbm.at[0, :, ends], e_raw.at[:, ends], 4 + k))
+
+    @pl.when(row == 0)
+    def _():
+        for copy in [get_b] + get_e + [get_c]:
+            copy.start()
+
+    @pl.when(row != 0)
+    def _():
+        for copy in [get_m] + get_e + [get_b, get_c, get_r]:
+            copy.start()
 
     barrier = pltpu.get_barrier_semaphore()
     pl.semaphore_signal(barrier, inc=1, device_id={"row": 1 - row})
@@ -122,7 +134,6 @@
         pl.semaphore_signal(barrier, inc=1, device_id={"col": lax.rem(col + d, cols)})
     for d in range(1, subs):
         pl.semaphore_signal(barrier, inc=1, device_id={"sub": lax.rem(sub + d, subs)})
-    pl.semaphore_wait(barrier, 1 + (cols - 1) + (subs - 1))
 
     def ahead(d):
         return lax.rem(col + d, cols)
@@ -143,48 +154,69 @@
             source, target, col_snd.at[stage, d], col_rcv.at[stage, d], device_id={"col": ahead(d)}
         )
 
+    def rows_of(piece, size):
+        return pl.ds(piece * (size // PIECES), size // PIECES)
+
+    def piece_of(k, piece, size):
+        extent = size // PIECES
+        return pl.ds(pl.multiple_of(k * size + piece * extent, extent), extent)
+
     def scatter(make, send, receive, stage):
+        size = send.shape[1]
+        own, copies = [], []
+        for piece in range(PIECES):
+            rows = rows_of(piece, size)
+            sent = []
+            for d in range(1, cols):
+                send[d, rows, :] = make(ahead(d), piece).astype(send.dtype)
+                copy = to_col(
+                    send.at[d, rows], receive.at[d, rows], stage * PIECES + piece, d
+                )
+                copy.start()
+                sent.append(copy)
+            own.append(make(col, piece))
+            copies.append(sent)
+        return own, copies
+
+    def gathered(own, receive, copies, piece):
+        total = own[piece]
+        rows = rows_of(piece, receive.shape[1])
+        for d, copy in zip(range(1, cols), copies[piece]):
+            copy.wait_recv()
+            total = total + receive[d, rows, :].astype(F32)
+        return total
+
+    def share_out(target, slot):
         copies = []
         for d in range(1, cols):
-            send[d] = make(ahead(d)).astype(send.dtype)
-            copy = to_col(send.at[d], receive.at[d], stage, d)
-            copy.start()
-            copies.append(copy)
-        return make(col), copies
-
-    def gathered(own, receive, copies):
-        for d, copy in zip(range(1, cols), copies):
-            copy.wait_recv()
-            own = own + receive[d].astype(F32)
-        return own
-
-    def share_out(buffer, place, stage):
-        copies = []
-        for d in range(1, cols):
-            copy = to_col(buffer.at[place], buffer.at[place], stage, d)
+            copy = to_col(target, target, slot, d)
             copy.start()
             copies.append(copy)
         return copies
 
     def finish(copies):
         for copy in copies:
-            copy.wait_send()
-
-    def split_inverse():
+            if isinstance(copy, list):
+                finish(copy)
+            else:
+                copy.wait_send()
+
+    def apply_inverse():
+        get_b.wait()
+        total = jnp.zeros((width, b_raw.shape[1]), F32)
         for k in range(cols):
-            e_hi[k], e_lo[k] = halves(e_raw[:, k * width : (k + 1) * width])
+            get_e[k].wait()
+            high, low = halves(e_raw[:, k * width : (k + 1) * width])
+            e_hi[k] = high
+            e_lo[k] = low
+            pair = paired(b_raw[k * width : (k + 1) * width, :])
+            total = total + mm_paired(high, low, pair)
+        return total
 
     def turn_inverse():
         for k in range(cols):
             et_hi[k], et_lo[k] = halves(e_raw[:, k * width : (k + 1) * width].T)
 
-    def apply_inverse():
-        total = jnp.zeros((width, b_raw.shape[1]), F32)
-        for k in range(cols):
-            pair = paired(b_raw[k * width : (k + 1) * width, :])
-            total = total + mm_paired(e_hi[k], e_lo[k], pair)
-        return total
-
     step = min(BLOCK, separator)
 
     def hits(first):
@@ -201,34 +233,9 @@
 
     @pl.when(row == 0)
     def _():
-        get_e.wait()
-        get_b.wait()
-        split_inverse()
         value = apply_inverse()
         y_keep[...] = value
         y_low[...] = value.astype(BF16)
-        first = to_pair(y_low, y_first, 0)
-        first.start()
-        get_c.wait()
-        make_spread()
-        mapped_snd[...] = mm(spread[...], y_low[...])
-        second = to_pair(mapped_snd, mapped_rcv, 1)
-        second.start()
-        make_spread_turn()
-        turn_inverse()
-        get_m.wait()
-        get_r.wait()
-        to_pair(sep_low, sep_low, 2).wait_recv()
-        y_keep[...] = y_keep[...] - mm(spread_turn[...], sep_low[...])
-        to_pair(root_keep, root_keep, 3).wait_recv()
-        root_out[...] = root_keep[...]
-        to_pair(give, take, 4).wait_recv()
-        pair = paired(y_keep[...] - take[...])
-        own, copies = scatter(
-            lambda k: mm_paired(et_hi[k], et_lo[k], pair), back_snd, back_rcv, 4
-        )
-        x_out[0] = gathered(own, back_rcv, copies)
-        finish(copies + [first, second])
 
     @pl.when(row != 0)
     def _():
@@ -245,102 +252,155 @@
             piece = m_raw[:, k * width : (k + 1) * width]
             m_mask[k] = piece
             m_turn[k] = piece.astype(F32).T.astype(BF16)
+
+    pl.semaphore_wait(barrier, 1 + (cols - 1) + (subs - 1))
+
+    def turned(pair):
+        def make(k, piece):
+            rows = rows_of(piece, width)
+            return mm_paired(et_hi[k, rows, :], et_lo[k, rows, :], pair)
+
+        return make
+
+    @pl.when(row == 0)
+    def _():
+        first = to_pair(y_low, y_first, 0)
+        first.start()
+        get_c.wait()
+        make_spread()
+        mapped_snd[...] = mm(spread[...], y_low[...])
+        second = to_pair(mapped_snd, mapped_rcv, 1)
+        second.start()
+        make_spread_turn()
+        turn_inverse()
+        to_pair(sep_low, sep_low, 2).wait_recv()
+        y_keep[...] = y_keep[...] - mm(spread_turn[...], sep_low[...])
+        to_pair(root_keep, root_keep, 3).wait_recv()
+        root_out[...] = root_keep[...]
+        to_pair(give, take, 4).wait_recv()
+        pair = paired(y_keep[...] - take[...])
+        own, copies = scatter(turned(pair), back_snd, back_rcv, 7)
+        for piece in range(PIECES):
+            x_out[0, rows_of(piece, width), :] = gathered(own, back_rcv, copies, piece)
+        finish(copies + [first, second])
+
+    @pl.when(row != 0)
+    def _():
         to_pair(y_low, y_first, 0).wait_recv()
         low = y_first[...]
-        own, sends_a = scatter(lambda k: mm(m_turn[k], low), a_snd, a_rcv, 0)
-        get_e.wait()
-        get_b.wait()
-        split_inverse()
+        own, sends_a = scatter(
+            lambda k, piece: mm(m_turn[k, rows_of(piece, width), :], low), a_snd, a_rcv, 0
+        )
         started = apply_inverse()
-        own = gathered(own, a_rcv, sends_a)
-        a_all[col] = own.astype(BF16)
-        sends_b = share_out(a_all, col, 1)
+        sends_b = []
+        for piece in range(PIECES):
+            rows = rows_of(piece, width)
+            a_all[col, rows, :] = gathered(own, a_rcv, sends_a, piece).astype(BF16)
+            sends_b.append(share_out(a_all.at[col, rows], PIECES + piece))
         get_c.wait()
         make_spread()
         value = started
         for d in range(cols):
             k = behind(d)
             if d > 0:
-                sends_b[d - 1].wait_recv()
+                for piece in range(PIECES):
+                    sends_b[piece][d - 1].wait_recv()
             value = value - (mm(e_hi[k], a_all[k]) + mm(e_lo[k], a_all[k]))
         y_keep[...] = value
-        y_low[...] = value.astype(BF16)
+        own_low = value.astype(BF16)
         to_pair(mapped_snd, mapped_rcv, 1).wait_recv()
-        own_low = y_low[...]
-        own, sends_c = scatter(
-            lambda k: mm(spread[part(k, share), :], own_low) + mapped_rcv[part(k, share), :],
-            s_snd,
-            s_rcv,
-            2,
-        )
+
+        def separator_rows(k, piece):
+            rows = piece_of(k, piece, share)
+            return mm(spread[rows, :], own_low) + mapped_rcv[rows, :]
+
+        own, sends_c = scatter(separator_rows, s_snd, s_rcv, 2)
         get_r.wait()
         r_hi[...], r_lo[...] = halves(r_raw[...])
         for first in range(0, separator, step):
             ends = slice(first, first + step)
             rt_hi[ends, :], rt_lo[ends, :] = halves(r_raw[:, ends].T)
-        own = gathered(own, s_rcv, sends_c)
-        z_snd[...] = own.astype(z_snd.dtype)
         sends_z = []
-        for d in range(1, subs):
-            copy = pltpu.make_async_remote_copy(
-                z_snd,
-                z_rcv.at[d],
-                z_ssem.at[d],
-                z_rsem.at[d],
-                device_id={"sub": lax.rem(sub + d, subs)},
-            )
-            copy.start()
-            sends_z.append(copy)
+        for piece in range(PIECES):
+            rows = rows_of(piece, share)
+            own[piece] = gathered(own, s_rcv, sends_c, piece)
+            z_snd[rows, :] = own[piece].astype(BF16)
+            sent = []
+            for d in range(1, subs):
+                copy = pltpu.make_async_remote_copy(
+                    z_snd.at[rows],
+                    z_rcv.at[d, rows],
+                    z_ssem.at[piece, d],
+                    z_rsem.at[piece, d],
+                    device_id={"sub": lax.rem(sub + d, subs)},
+                )
+                copy.start()
+                sent.append(copy)
+            sends_z.append(sent)
         make_spread_turn()
         turn_inverse()
-        for d, copy in zip(range(1, subs), sends_z):
+        sends_d = []
+        for piece in range(PIECES):
+            rows = rows_of(piece, share)
+            total = own[piece]
+            for d, copy in zip(range(1, subs), sends_z[piece]):
+                copy.wait_recv()
+                total = total + z_rcv[d, rows, :].astype(F32)
+            high, low = halves(root_right[rows, :] - total)
+            place = piece_of(col, piece, share)
+            rhs_hi[place, :] = high
+            rhs_lo[place, :] = low
+            sends_d.append(share_out(rhs_hi.at[place], 3 * PIECES + piece))
+        rest = share_out(rhs_lo.at[part(col, share)], 4 * PIECES)
+        for sent in sends_d:
+            for copy in sent:
+                copy.wait_recv()
+        half = mm(r_hi[...], rhs_hi[...]) + mm(r_lo[...], rhs_hi[...])
+        for copy in rest:
             copy.wait_recv()
-            own = own + z_rcv[d].astype(F32)
-        rhs_all[part(col, share), :] = (root_right[...] - own).astype(rhs_all.dtype)
-        sends_d = share_out(rhs_all, part(col, share), 3)
-        for copy in sends_d:
-            copy.wait_recv()
-        if rhs_all.dtype == BF16:
-            half = mm(r_hi[...], rhs_all[...]) + mm(r_lo[...], rhs_all[...])
-        else:
-            half = mm_paired(r_hi[...], r_lo[...], paired(rhs_all[...]))
-        pair_r = paired(half)
-        own, sends_e = scatter(
-            lambda k: mm_paired(rt_hi[part(k, share), :], rt_lo[part(k, share), :], pair_r),
-            t_snd,
-            t_rcv,
-            5,
-        )
-        own = gathered(own, t_rcv, sends_e)
-        sep_low[part(col, share), :] = own.astype(BF16)
-        sends_f = share_out(sep_low, part(col, share), 6)
-        root_out[...] = own
-        root_keep[...] = own
+        pair_r = paired(half + mm(r_hi[...], rhs_lo[...]))
+
+        def root_rows(k, piece):
+            rows = piece_of(k, piece, share)
+            return mm_paired(rt_hi[rows, :], rt_lo[rows, :], pair_r)
+
+        own, sends_e = scatter(root_rows, t_snd, t_rcv, 5)
+        sends_f = []
+        for piece in range(PIECES):
+            total = gathered(own, t_rcv, sends_e, piece)
+            place = piece_of(col, piece, share)
+            sep_low[place, :] = total.astype(BF16)
+            sends_f.append(share_out(sep_low.at[place], 6 * PIECES + piece))
+            root_out[rows_of(piece, share), :] = total
+            root_keep[rows_of(piece, share), :] = total
         third = to_pair(root_keep, root_keep, 3)
         third.start()
-        for copy in sends_f:
-            copy.wait_recv()
+        for sent in sends_f:
+            for copy in sent:
+                copy.wait_recv()
         fourth = to_pair(sep_low, sep_low, 2)
         fourth.start()
         pair = paired(y_keep[...] - mm(spread_turn[...], sep_low[...]))
-        own, sends_g = scatter(
-            lambda k: mm_paired(et_hi[k], et_lo[k], pair), back_snd, back_rcv, 4
-        )
-        own = gathered(own, back_rcv, sends_g)
-        x_all[col] = own.astype(BF16)
-        sends_h = share_out(x_all, col, 7)
-        x_out[0] = own
-        total = jnp.zeros((width, own.shape[1]), F32)
+        own, sends_g = scatter(turned(pair), back_snd, back_rcv, 7)
+        sends_h = []
+        for piece in range(PIECES):
+            rows = rows_of(piece, width)
+            total = gathered(own, back_rcv, sends_g, piece)
+            x_all[col, rows, :] = total.astype(BF16)
+            sends_h.append(share_out(x_all.at[col, rows], 8 * PIECES + piece))
+            x_out[0, rows, :] = total
+        total = jnp.zeros(give.shape, F32)
         for d in range(cols):
             k = behind(d)
             if d > 0:
-                sends_h[d - 1].wait_recv()
+                for piece in range(PIECES):
+                    sends_h[piece][d - 1].wait_recv()
             total = total + mm(m_mask[k], x_all[k])
         give[...] = total
         fifth = to_pair(give, take, 4)
         fifth.start()
-        finish(sends_a + sends_b + sends_c + sends_z + sends_d + sends_e + sends_f + sends_g)
-        finish(sends_h + [third, fourth, fifth])
+        finish([sends_a, sends_b, sends_c, sends_z, sends_d, rest, sends_e, sends_f])
+        finish([sends_g, sends_h, third, fourth, fifth])
 
 
 def shards(
@@ -394,7 +454,8 @@
         V((cols, share, sources), BF16),
         V((share, sources), BF16),
         V((subs, share, sources), BF16),
-        V((separator, sources), ROOT_TYPE),
+        V((separator, sources), BF16),
+        V((separator, sources), BF16),
         V((cols, share, sources), BF16),
         V((cols, share, sources), BF16),
         V((separator, sources), BF16),
@@ -404,13 +465,13 @@
         V((cols, width, sources), BF16),
         V((width, sources), F32),
         V((width, sources), F32),
+        pltpu.SemaphoreType.DMA((4 + cols,)),
         pltpu.SemaphoreType.DMA((5,)),
         pltpu.SemaphoreType.DMA((5,)),
-        pltpu.SemaphoreType.DMA((5,)),
-        pltpu.SemaphoreType.DMA((8, cols)),
-        pltpu.SemaphoreType.DMA((8, cols)),
-        pltpu.SemaphoreType.DMA((subs,)),
-        pltpu.SemaphoreType.DMA((subs,)),
+        pltpu.SemaphoreType.DMA((10 * PIECES, cols)),
+        pltpu.SemaphoreType.DMA((10 * PIECES, cols)),
+        pltpu.SemaphoreType.DMA((PIECES, subs)),
+        pltpu.SemaphoreType.DMA((PIECES, subs)),
     ]
     return pl.pallas_call(
         functools.partial(kernel, sizes),

time: 69.3 us -> 67.1 us (0.968)
  Pallas kernels: 65.2 us -> 62.9 us
    pallas_call x1, Pallas kernels: 65.2 us -> 62.9 us  [shards(): pl.pallas_call(functools.partial(kernel, sizes), out_shape=(jax.ShapeDtyp...]
where the time goes in v2:
time: 67.1 us; the launch traced here: 66.9 us
  Pallas kernels  62.9 us (94%)
  local copies, waits for them, and re-layouts  3.29 us (5%)
    pallas_call x1, Pallas kernels, shards(): pl.pallas_call(functools.partial(kernel, sizes), out_shape=(jax.ShapeDtyp...  62.9 us
    unnamed x2, local copies, waits for them, and re-layouts  3.29 us

profile of v2, /device:TPU:0, one launch (start us, length us, event | category | flops | bytes accessed | tf_op | source)
XLA Modules:
  0.0 66.9 jit_solution(3016005085684765789)
XLA Ops:
  0.6 62.9 %tree_solve.1 = (f32[1,512,128]{2,1,0:T(8,128)}, f32[384,128]{1,0:T(8,128)}) custom-call(bf16[1,2,512,2048]{3,2,1,0:T(8,128)(2,1)} %factor_hbm.1, s32[1,16,16]{2,1,0:T(8,128)} %pattern.1, f32[1,512,2048]{2,1,0:T(8,128)} %inverse_hbm.1, bf16[1,1,512,1024]{3,2,1,0:T(8,128)(2,1)} %couple_hbm.1, s32[1,1024]{1,0:T(1,128)} %rows_ref.1, f32[384,1536]{1,0:T(8,128)} %root_hbm.1, ...), custom_call_target="tpu_custom_call" | custom-call | tf_op jit(solution)/shard_map/tree_solve/pallas_call | solution.py:476
  63.6 1.7 %copy.12 = f32[1,512,128]{2,1,0:T(8,128)} copy(f32[1,512,128]{2,1,0:T(8,128)} %get-tuple-element.4) | data formatting | bytes 524288
  65.2 1.6 %copy.13 = f32[384,128]{1,0:T(8,128)} copy(f32[384,128]{1,0:T(8,128)} %get-tuple-element.5) | data formatting | bytes 393216

commit v3 on v2

--- a/solution.py
+++ b/solution.py
@@ -40,15 +40,18 @@
 def kernel(
     sizes,
     factor_hbm,
-    pattern,
+    pattern_hbm,
     inverse_hbm,
     couple_hbm,
-    rows_ref,
+    rows_hbm,
     root_hbm,
     right_hbm,
-    root_right,
+    root_right_hbm,
     x_out,
     root_out,
+    pattern,
+    rows_ref,
+    root_right,
     e_raw,
     m_raw,
     c_raw,
@@ -113,6 +116,9 @@
     get_m = load(factor_hbm.at[0, 0], m_raw, 1)
     get_c = load(couple_hbm.at[0, 0], c_raw, 2)
     get_r = load(root_hbm, r_raw, 3)
+    get_p = load(pattern_hbm, pattern, 4 + cols)
+    get_s = load(rows_hbm, rows_ref, 5 + cols)
+    get_t = load(root_right_hbm, root_right, 6 + cols)
     get_e = []
     for k in range(cols):
         ends = pl.ds(k * width, width)
@@ -120,12 +126,12 @@
 
     @pl.when(row == 0)
     def _():
-        for copy in [get_b] + get_e + [get_c]:
+        for copy in [get_b] + get_e + [get_c, get_s]:
             copy.start()
 
     @pl.when(row != 0)
     def _():
-        for copy in [get_m] + get_e + [get_b, get_c, get_r]:
+        for copy in [get_p, get_m] + get_e + [get_b, get_c, get_s, get_r, get_t]:
             copy.start()
 
     barrier = pltpu.get_barrier_semaphore()
@@ -135,11 +141,19 @@
     for d in range(1, subs):
         pl.semaphore_signal(barrier, inc=1, device_id={"sub": lax.rem(sub + d, subs)})
 
-    def ahead(d):
-        return lax.rem(col + d, cols)
-
-    def behind(d):
-        return lax.rem(col + cols - d, cols)
+    def partner(place, d):
+        bit = 1
+        while bit <= d:
+            if d & bit:
+                place = place + bit * (1 - 2 * (place // bit % 2))
+            bit *= 2
+        return place
+
+    def other(d):
+        return partner(col, d)
+
+    order = tuple(range(cols - 1, 0, -1))
+    arrival = (0,) + tuple(range(cols // 2, cols - 1)) + tuple(range(1, cols // 2)) + (cols - 1,)
 
     def part(k, size):
         return pl.ds(pl.multiple_of(k * size, size), size)
@@ -151,7 +165,7 @@
 
     def to_col(source, target, stage, d):
         return pltpu.make_async_remote_copy(
-            source, target, col_snd.at[stage, d], col_rcv.at[stage, d], device_id={"col": ahead(d)}
+            source, target, col_snd.at[stage, d], col_rcv.at[stage, d], device_id={"col": other(d)}
         )
 
     def rows_of(piece, size):
@@ -167,8 +181,8 @@
         for piece in range(PIECES):
             rows = rows_of(piece, size)
             sent = []
-            for d in range(1, cols):
-                send[d, rows, :] = make(ahead(d), piece).astype(send.dtype)
+            for d in order:
+                send[d, rows, :] = make(other(d), piece).astype(send.dtype)
                 copy = to_col(
                     send.at[d, rows], receive.at[d, rows], stage * PIECES + piece, d
                 )
@@ -181,14 +195,14 @@
     def gathered(own, receive, copies, piece):
         total = own[piece]
         rows = rows_of(piece, receive.shape[1])
-        for d, copy in zip(range(1, cols), copies[piece]):
+        for d, copy in zip(order, copies[piece]):
             copy.wait_recv()
             total = total + receive[d, rows, :].astype(F32)
         return total
 
     def share_out(target, slot):
         copies = []
-        for d in range(1, cols):
+        for d in order:
             copy = to_col(target, target, slot, d)
             copy.start()
             copies.append(copy)
@@ -240,6 +254,7 @@
     @pl.when(row != 0)
     def _():
         tall = min(width, BLOCK)
+        get_p.wait()
         get_m.wait()
         for at in range(0, width, tall):
             column = (col * width + at) // BLOCK
@@ -267,6 +282,7 @@
         first = to_pair(y_low, y_first, 0)
         first.start()
         get_c.wait()
+        get_s.wait()
         make_spread()
         mapped_snd[...] = mm(spread[...], y_low[...])
         second = to_pair(mapped_snd, mapped_rcv, 1)
@@ -298,13 +314,14 @@
             a_all[col, rows, :] = gathered(own, a_rcv, sends_a, piece).astype(BF16)
             sends_b.append(share_out(a_all.at[col, rows], PIECES + piece))
         get_c.wait()
+        get_s.wait()
         make_spread()
         value = started
-        for d in range(cols):
-            k = behind(d)
+        for d in arrival:
+            k = other(d)
             if d > 0:
                 for piece in range(PIECES):
-                    sends_b[piece][d - 1].wait_recv()
+                    sends_b[piece][order.index(d)].wait_recv()
             value = value - (mm(e_hi[k], a_all[k]) + mm(e_lo[k], a_all[k]))
         y_keep[...] = value
         own_low = value.astype(BF16)
@@ -316,36 +333,49 @@
 
         own, sends_c = scatter(separator_rows, s_snd, s_rcv, 2)
         get_r.wait()
+        get_t.wait()
         r_hi[...], r_lo[...] = halves(r_raw[...])
         for first in range(0, separator, step):
             ends = slice(first, first + step)
             rt_hi[ends, :], rt_lo[ends, :] = halves(r_raw[:, ends].T)
+        rounds = subs.bit_length() - 1
         sends_z = []
-        for piece in range(PIECES):
+
+        def exchange(total, piece, level):
             rows = rows_of(piece, share)
+            z_snd[level, rows, :] = total.astype(BF16)
+            copy = pltpu.make_async_remote_copy(
+                z_snd.at[level, rows],
+                z_rcv.at[level, rows],
+                z_ssem.at[piece, level],
+                z_rsem.at[piece, level],
+                device_id={"sub": partner(sub, 1 << level)},
+            )
+            copy.start()
+            sends_z.append(copy)
+            return copy
+
+        def received(total, copy, piece, level):
+            copy.wait_recv()
+            return total + z_rcv[level, rows_of(piece, share), :].astype(F32)
+
+        flying = []
+        for piece in range(PIECES):
             own[piece] = gathered(own, s_rcv, sends_c, piece)
-            z_snd[rows, :] = own[piece].astype(BF16)
-            sent = []
-            for d in range(1, subs):
-                copy = pltpu.make_async_remote_copy(
-                    z_snd.at[rows],
-                    z_rcv.at[d, rows],
-                    z_ssem.at[piece, d],
-                    z_rsem.at[piece, d],
-                    device_id={"sub": lax.rem(sub + d, subs)},
-                )
-                copy.start()
-                sent.append(copy)
-            sends_z.append(sent)
+            if rounds:
+                flying.append(exchange(own[piece], piece, 0))
         make_spread_turn()
-        turn_inverse()
+        for level in range(rounds):
+            for piece in range(PIECES):
+                own[piece] = received(own[piece], flying[piece], piece, level)
+                if level + 1 < rounds:
+                    flying[piece] = exchange(own[piece], piece, level + 1)
+            if level == 0:
+                turn_inverse()
         sends_d = []
         for piece in range(PIECES):
             rows = rows_of(piece, share)
             total = own[piece]
-            for d, copy in zip(range(1, subs), sends_z[piece]):
-                copy.wait_recv()
-                total = total + z_rcv[d, rows, :].astype(F32)
             high, low = halves(root_right[rows, :] - total)
             place = piece_of(col, piece, share)
             rhs_hi[place, :] = high
@@ -390,17 +420,22 @@
             sends_h.append(share_out(x_all.at[col, rows], 8 * PIECES + piece))
             x_out[0, rows, :] = total
         total = jnp.zeros(give.shape, F32)
-        for d in range(cols):
-            k = behind(d)
+        for d in arrival:
+            k = other(d)
             if d > 0:
                 for piece in range(PIECES):
-                    sends_h[piece][d - 1].wait_recv()
+                    sends_h[piece][order.index(d)].wait_recv()
             total = total + mm(m_mask[k], x_all[k])
         give[...] = total
         fifth = to_pair(give, take, 4)
         fifth.start()
         finish([sends_a, sends_b, sends_c, sends_z, sends_d, rest, sends_e, sends_f])
         finish([sends_g, sends_h, third, fourth, fifth])
+
+
+def write_out(x_ref, root_ref, x_out, root_out):
+    x_out[...] = x_ref[...]
+    root_out[...] = root_ref[...]
 
 
 def shards(
@@ -421,10 +456,12 @@
     coupled = coupling_cols.shape[3]
     hbm = pl.BlockSpec(memory_space=pl.ANY)
     vmem = pl.BlockSpec(memory_space=pltpu.VMEM)
-    smem = pl.BlockSpec(memory_space=pltpu.SMEM)
     V = pltpu.VMEM
     tile = (cols, width, width)
     scratch = [
+        pltpu.SMEM(block_pattern.shape, jnp.int32),
+        V(separator_rows.shape, jnp.int32),
+        V(root_right.shape, F32),
         V((width, panel), F32),
         V((width, panel), BF16),
         V((width, coupled), BF16),
@@ -452,7 +489,7 @@
         V((cols, width, sources), BF16),
         V((cols, share, sources), BF16),
         V((cols, share, sources), BF16),
-        V((share, sources), BF16),
+        V((subs, share, sources), BF16),
         V((subs, share, sources), BF16),
         V((separator, sources), BF16),
         V((separator, sources), BF16),
@@ -465,7 +502,7 @@
         V((cols, width, sources), BF16),
         V((width, sources), F32),
         V((width, sources), F32),
-        pltpu.SemaphoreType.DMA((4 + cols,)),
+        pltpu.SemaphoreType.DMA((7 + cols,)),
         pltpu.SemaphoreType.DMA((5,)),
         pltpu.SemaphoreType.DMA((5,)),
         pltpu.SemaphoreType.DMA((10 * PIECES, cols)),
@@ -473,13 +510,13 @@
         pltpu.SemaphoreType.DMA((PIECES, subs)),
         pltpu.SemaphoreType.DMA((PIECES, subs)),
     ]
-    return pl.pallas_call(
+    solved = pl.pallas_call(
         functools.partial(kernel, sizes),
         out_shape=(
             jax.ShapeDtypeStruct((1, width, sources), F32),
             jax.ShapeDtypeStruct((share, sources), F32),
         ),
-        in_specs=[hbm, smem, hbm, hbm, vmem, hbm, hbm, vmem],
+        in_specs=[hbm] * 8,
         out_specs=(vmem, vmem),
         scratch_shapes=scratch,
         compiler_params=pltpu.CompilerParams(
@@ -496,6 +533,13 @@
         right_side,
         root_right,
     )
+    return pl.pallas_call(
+        write_out,
+        out_shape=tuple(jax.ShapeDtypeStruct(a.shape, a.dtype) for a in solved),
+        in_specs=[vmem, vmem],
+        out_specs=(vmem, vmem),
+        name="write_out",
+    )(*solved)
 
 
 def solution(mesh):

time: 67.1 us -> 67.7 us (level)
  Pallas kernels: 62.9 us -> 66.9 us
  local copies, waits for them, and re-layouts: 3.29 us -> 0 us
    unnamed x2 -> x0, local copies, waits for them, and re-layouts: 3.29 us -> none
    pallas_call x1, Pallas kernels: 62.9 us -> 65.1 us  [shards(): pl.pallas_call(functools.partial(kernel, sizes), out_shape=(jax.ShapeDtyp...]
    pallas_call x0 -> x1, Pallas kernels: none -> 1.79 us  [shards(): pl.pallas_call(write_out, out_shape=tuple((jax.ShapeDtypeStruct(a.shape,...]
where the time goes in v3:
time: 67.7 us; the launch traced here: 67.6 us
  Pallas kernels  66.9 us (99%)
    pallas_call x1, Pallas kernels, shards(): pl.pallas_call(functools.partial(kernel, sizes), out_shape=(jax.ShapeDtyp...  65.1 us
    pallas_call x1, Pallas kernels, shards(): pl.pallas_call(write_out, out_shape=tuple((jax.ShapeDtypeStruct(a.shape,...  1.79 us

profile of v3, /device:TPU:0, one launch (start us, length us, event | category | flops | bytes accessed | tf_op | source)
XLA Modules:
  0.0 67.6 jit_solution(8324259394858148462)
XLA Ops:
  0.6 65.1 %tree_solve.1 = (f32[1,512,128]{2,1,0:T(8,128)}, f32[384,128]{1,0:T(8,128)}) custom-call(bf16[1,2,512,2048]{3,2,1,0:T(8,128)(2,1)} %factor_hbm.1, s32[1,16,16]{2,1,0:T(8,128)} %pattern_hbm.1, f32[1,512,2048]{2,1,0:T(8,128)} %inverse_hbm.1, bf16[1,1,512,1024]{3,2,1,0:T(8,128)(2,1)} %couple_hbm.1, s32[1,1024]{1,0:T(1,128)} %rows_hbm.1, f32[384,1536]{1,0:T(8,128)} %root_hbm.1, ...), custom_call_target="tpu_custom_call" | custom-call | tf_op jit(solution)/shard_map/tree_solve/pallas_call | solution.py:513
  65.8 1.8 %write_out.1 = (f32[1,512,128]{2,1,0:T(8,128)}, f32[384,128]{1,0:T(8,128)}) custom-call(f32[1,512,128]{2,1,0:T(8,128)} %get-tuple-element.4.x_ref, f32[384,128]{1,0:T(8,128)} %get-tuple-element.5.root_ref), custom_call_target="tpu_custom_call" | custom-call | tf_op jit(solution)/shard_map/write_out/pallas_call | solution.py:536
